TPU v7x, 128 devices: a whole 4x4x4 slice. The times are simulated.
128 devices in a mesh: row: 8 (over y, z_lo), col: 16 (over x, z_hi, core).
Axes of the slice: x: 4, y: 4, z: 4 (z_hi: 2, z_lo: 2; z = z_hi * 2 + z_lo), core: 2. Of those that a mesh axis runs over, the one named last changes fastest.
Arguments:
- eigvecs: float32 [512, 65536], P(('col', 'row')), may hold values from -6 to 6
- row_map: int32 [65536], replicated, may hold values from 0 to 65535, as said below
- reflectors: float32 [16, 512, 65536], P(None, 'col', 'row'), may hold values from -0.0234375 to 0.0234375
- panel_factor: float32 [2, 512, 512], replicated, may hold values from -4 to 4
- owners: int32 [16], replicated, may hold values from 0 to 15, each once
Outputs:
- back_vectors: float32 [512, 65536], P('col', 'row')
Inputs may be any that keep to these rules, and one draw needn't show every extreme that they name: row_map is a permutation of 0 to 65535 that moves aligned blocks of 64 rows whole, keeping the order inside a block. owners is a permutation; only its first 2 entries are read, so only those slots of reflectors are used.
All inputs are finite; a program needn't handle non-finite values.
Results may differ from a plain program's by a relative error of at most 0.0001.
Values sent between devices are 32-bit elements; how exact they have to be, the bound alone decides.
A program may use at most 128 MiB of HBM per device.

v0:
```python
import jax
import jax.numpy as jnp
from jax import lax
from jax.sharding import PartitionSpec as P

PANELS = 2
NB = 64


def from_everyone(x, axis):
    copies = jnp.broadcast_to(x, (lax.axis_size(axis), *x.shape))
    return lax.all_to_all(copies, axis, split_axis=0, concat_axis=0, tiled=True)


def taken_together(x, axis):
    return from_everyone(x, axis).sum(axis=0)


def hdot(left, right):
    return jnp.dot(left, right, precision=lax.Precision.HIGHEST, preferred_element_type=jnp.float32)


def per_device(eigvecs, row_map, reflectors, panel_factor, owners):
    row_count = lax.axis_size("row")
    eig_local = eigvecs.shape[0]
    total_rows = eigvecs.shape[1]
    local_rows = total_rows // row_count
    block_count = total_rows // NB
    block_index = row_map.reshape(block_count, NB)[:, 0] // NB
    blocked = eigvecs.reshape(eig_local, block_count, NB)
    ordered = jnp.take(blocked, block_index, axis=1).reshape(eig_local, row_count, local_rows)
    arrived = lax.all_to_all(ordered, "row", split_axis=1, concat_axis=0, tiled=True)
    current = arrived.reshape(eig_local * row_count, local_rows)
    for panel in range(PANELS):
        vectors = lax.all_gather(reflectors[owners[panel]], "col", axis=0, tiled=True)
        upper = jnp.triu(panel_factor[panel])
        project = taken_together(hdot(current, vectors.T), "row")
        scaled = hdot(project, upper.T)
        current = current - hdot(scaled, vectors)
    return current


def solution(mesh):
    placed = (P(("col", "row"), None), P(), P(None, "col", "row"), P(), P())
    return jax.shard_map(
        per_device, mesh=mesh, in_specs=placed, out_specs=P("col", "row"), check_vma=False
    )
```

profile of v0, /device:TPU:0, one launch (start us, length us, event | category | flops | bytes accessed | tf_op | source)
XLA Modules:
  0.0 297.6 jit_solution(3470367636473523635)
XLA Ops:
  6.5 1.3 fusion.26
  11.5 3.0 %constant_dynamic-slice_fusion = (f32[1,32,8192]{2,1,0:T(8,128)}, f32[1,32,8192]{2,1,0:T(8,128)}) fusion(f32[16,32,8192]{2,1,0:T(8,128)} %param.7, s32[]{:T(128)S(6)} %select_n.36, s32[]{:T(128)S(6)} %select_n.34), kind=kLoop, calls=%fused_computation.34 | loop fusion | bytes 4194312 | tf_op jit(solution)/shard_map/dynamic_slice | solution.py:35
  14.5 0.0 all-gather.7.cloned.1.call-start
  14.6 0.7 all-gather.7.cloned.1.call-update
  15.3 3.5 %reshape.21 = f32[4,1024,64]{2,1,0:T(8,128)} reshape(f32[4,65536]{1,0:T(4,128)} %param.5) | data formatting | bytes 2097152 | tf_op jit(solution)/shard_map/reshape | solution.py:30
  18.8 2.9 copy.15
  21.8 1.1 reshape.20
  22.9 0.5 and_reduce_fusion
  23.4 0.2 reduce.1
  23.6 7.9 %gather_fusion = f32[1024,4,64]{2,1,0:T(4,128)} fusion(f32[4,1024,64]{2,0,1:T(4,128)S(1)} %copy.15, s32[1024]{0:T(1024)S(1)} %broadcast_clamp_fusion), kind=kCustom, calls=%fused_computation | custom fusion | bytes 2101248 | tf_op jit(solution)/shard_map/jit(_take)/gather | solution.py:31
  31.6 1.7 copy.16
  33.3 0.7 gather.7
  33.9 0.2 broadcast_in_dim.28
  34.2 0.2 broadcast_in_dim.29
  34.4 0.1 broadcast_select_fusion
  34.5 0.7 copy.17
  35.2 21.1 %all_to_all.25 = f32[4,8,8192]{2,0,1:T(4,128)S(1)} all-to-all(f32[4,8,8192]{2,0,1:T(4,128)S(1)} %copy.17), channel_id=1, replica_groups=mesh['row'=8,'col'=16] {'row'}, dimensions={1} | all-to-all | bytes 2097152 | tf_op jit(solution)/shard_map/all_to_all | solution.py:32
  56.3 0.4 reshape.22
  56.6 70.3 %all-gather.5.cloned.1.call-done = f32[1,512,8192]{2,1,0:T(8,128)} async-done(((f32[1,32,8192]{2,1,0:T(8,128)}), f32[1,512,8192]{2,1,0:T(8,128)}) %all-gather.5.cloned.1.call-update) | async-done | bytes 16777232 | tf_op jit(solution)/shard_map/all_gather | solution.py:35
  126.9 18.1 %fusion.6 = f32[32,512]{1,0:T(8,128)S(1)} fusion(f32[32,8192]{1,0:T(8,128)S(1)} %reshape.22, f32[1,512,8192]{2,1,0:T(8,128)} %all-gather.5.cloned.1.call-done), kind=kOutput, calls=%fused_computation.7 | convolution fusion | flops 1610612736 | bytes 17891328 | tf_op jit(solution)/shard_map/dot_general | solution.py:20
  145.1 0.9 broadcast_in_dim.32
  146.0 4.4 %all-to-all-start.1 = ((f32[8,32,512]{2,1,0:T(8,128)}), f32[8,32,512]{2,1,0:T(8,128)}, u32[]{:S(2)}, u32[]{:S(2)}) async-start(f32[8,32,512]{2,1,0:T(8,128)} %broadcast_in_dim.32), calls=%async_computation.1 | async-start | bytes 1048576 | tf_op jit(solution)/shard_map/all_to_all | solution.py:12
  150.3 10.0 %all-to-all-done.1 = f32[8,32,512]{2,1,0:T(8,128)} async-done(((f32[8,32,512]{2,1,0:T(8,128)}), f32[8,32,512]{2,1,0:T(8,128)}, u32[]{:S(2)}, u32[]{:S(2)}) %all-to-all-start.1) | async-done | bytes 524320 | tf_op jit(solution)/shard_map/all_to_all | solution.py:12
  160.3 1.1 reduce_sum.18
  161.4 1.2 fusion.15
  162.6 13.1 %fusion.8 = f32[32,8192]{1,0:T(8,128)S(1)} fusion(f32[32,8192]{1,0:T(8,128)S(1)} %reshape.22, f32[32,512]{1,0:T(8,128)S(1)} %fusion.15, f32[1,512,8192]{2,1,0:T(8,128)} %all-gather.5.cloned.1.call-done), kind=kOutput, calls=%fused_computation.9 | convolution fusion | flops 1610874880 | bytes 18939904 | tf_op jit(solution)/shard_map/dot_general | solution.py:20
  175.7 65.9 %all-gather.7.cloned.1.call-done = f32[1,512,8192]{2,1,0:T(8,128)} async-done(((f32[1,32,8192]{2,1,0:T(8,128)}), f32[1,512,8192]{2,1,0:T(8,128)}) %all-gather.7.cloned.1.call-update) | async-done | bytes 16777232 | tf_op jit(solution)/shard_map/all_gather | solution.py:35
  241.6 18.1 %fusion.2 = f32[32,512]{1,0:T(8,128)S(1)} fusion(f32[32,8192]{1,0:T(8,128)S(1)} %fusion.8, f32[1,512,8192]{2,1,0:T(8,128)} %all-gather.7.cloned.1.call-done), kind=kOutput, calls=%fused_computation.3 | convolution fusion | flops 1610612736 | bytes 17891328 | tf_op jit(solution)/shard_map/dot_general | solution.py:20
  259.7 0.1 broadcast_in_dim.34
  259.8 14.3 %all_to_all.26 = f32[8,32,512]{2,1,0:T(8,128)S(1)} all-to-all(f32[8,32,512]{2,1,0:T(8,128)S(1)} %broadcast_in_dim.34), channel_id=1, replica_groups=mesh['row'=8,'col'=16] {'row'}, dimensions={0} | all-to-all | bytes 1048576 | tf_op jit(solution)/shard_map/all_to_all | solution.py:12
  274.2 2.4 fusion.14
  276.5 14.2 %fusion.11 = f32[32,8192]{1,0:T(8,128)} fusion(f32[32,8192]{1,0:T(8,128)S(1)} %fusion.8, f32[32,512]{1,0:T(8,128)S(1)} %fusion.14, f32[1,512,8192]{2,1,0:T(8,128)} %all-gather.7.cloned.1.call-done), kind=kOutput, calls=%fused_computation.10 | convolution fusion | flops 1610874880 | bytes 18939904 | tf_op jit(solution)/shard_map/dot_general | solution.py:20
  (7 shorter events, 0.1 us)
Async XLA Ops:
  6.5 120.4 %all-gather.5.cloned.1.call-start = ((), (), s32[]{:S(2)}) async-start(), calls=%async_computation.3 | async-start | bytes 17825792 | tf_op jit(solution)/shard_map/all_gather | solution.py:35
  14.5 227.1 %all-gather.7.cloned.1.call-start = ((), (), s32[]{:S(2)}) async-start(), calls=%async_computation.4 | async-start | bytes 17825792 | tf_op jit(solution)/shard_map/all_gather | solution.py:35
  56.6 104.8 %copy-start = (f32[2,512,512]{2,1,0:T(8,128)S(1)}, f32[2,512,512]{2,1,0:T(8,128)}, u32[]{:S(2)}) copy-start(f32[2,512,512]{2,1,0:T(8,128)} %param.8) | copy-start | bytes 6291460
  146.0 14.4 %all-to-all-start.1 = ((f32[8,32,512]{2,1,0:T(8,128)}), f32[8,32,512]{2,1,0:T(8,128)}, u32[]{:S(2)}, u32[]{:S(2)}) async-start(f32[8,32,512]{2,1,0:T(8,128)} %broadcast_in_dim.32), calls=%async_computation.1 | async-start | bytes 1048576 | tf_op jit(solution)/shard_map/all_to_all | solution.py:12
Sparse Core Ops, SparseCore 0:
  14.6 112.2 all-gather.4
  129.3 112.2 all-gather.6
where the time goes:
time: 298 us
  waiting for transfers between devices  147 us (49%)
  matrix products  67.1 us (23%)
  blocking collectives  35.4 us (12%)
  local copies, waits for them, and re-layouts  24.7 us (8%)
  between operations  17.1 us (6%)
  starting transfers between devices  4.43 us (1%)
    all_gather x2, waiting for transfers between devices, per_device(): lax.all_gather(reflectors[owners[panel]], 'col', axis=0, tiled=True)  136 us
    dot_general x6, matrix products, hdot(): jnp.dot(left, right, precision=lax.Precision.HIGHEST, preferred_element_t...  67.1 us
    all_to_all x1, blocking collectives, per_device(): lax.all_to_all(ordered, 'row', split_axis=1, concat_axis=0, tiled=True)  21.1 us
    all_to_all x1, blocking collectives, from_everyone(): return lax.all_to_all(copies, axis, split_axis=0, concat_axis=0, tiled=True)  14.3 us
    gather x3, local copies, waits for them, and re-layouts, per_device(): jnp.take(blocked, block_index, axis=1)  10.3 us
    all_to_all x1, waiting for transfers between devices, from_everyone(): return lax.all_to_all(copies, axis, split_axis=0, concat_axis=0, tiled=True)  9.99 us
    reshape x2, local copies, waits for them, and re-layouts, per_device(): blocked = eigvecs.reshape(eig_local, block_count, NB)  6.48 us
  transfers between devices with their start and end apart: 3, of which 3 were waited for; matrix products, arithmetic and copies ran while one was open for 18% of the time, Pallas kernels for 0%

commit v1 on v0

--- a/solution.py
+++ b/solution.py
@@ -32,7 +32,12 @@
     arrived = lax.all_to_all(ordered, "row", split_axis=1, concat_axis=0, tiled=True)
     current = arrived.reshape(eig_local * row_count, local_rows)
     for panel in range(PANELS):
-        vectors = lax.all_gather(reflectors[owners[panel]], "col", axis=0, tiled=True)
+        vectors = jnp.concatenate(
+            lax.all_to_all(
+                jnp.stack([reflectors[owners[panel]]] * lax.axis_size("col")), "col", 0, 0
+            ),
+            axis=0,
+        )
         upper = jnp.triu(panel_factor[panel])
         project = taken_together(hdot(current, vectors.T), "row")
         scaled = hdot(project, upper.T)

time: 298 us -> 697 us (2.34)
  waiting for transfers between devices: 147 us -> 535 us
  starting transfers between devices: 4.43 us -> 22.6 us
  local copies, waits for them, and re-layouts: 24.7 us -> 38.3 us
  between operations: 17.1 us -> 3.91 us
  blocking collectives: 35.4 us -> 25.4 us
    all_to_all x1 -> x3, waiting for transfers between devices: 9.99 us -> 535 us  [the longest x2 525 us: per_device(): lax.all_to_all(jnp.stack([reflectors[owners[panel]]] * lax.axis_size('col...]
    all_gather x2 -> x0, waiting for transfers between devices: 136 us -> none  [per_device(): lax.all_gather(reflectors[owners[panel]], 'col', axis=0, tiled=True)]
    all_to_all x1 -> x0, blocking collectives: 21.1 us -> none  [per_device(): lax.all_to_all(ordered, 'row', split_axis=1, concat_axis=0, tiled=True)]
    all_to_all x1 -> x3, starting transfers between devices: 4.38 us -> 22.6 us  [the longest x2 16.7 us: per_device(): lax.all_to_all(jnp.stack([reflectors[owners[panel]]] * lax.axis_size('col...]
    another operation x0 -> x2, local copies, waits for them, and re-layouts: none -> 15.5 us  [per_device(): jnp.stack([reflectors[owners[panel]]] * lax.axis_size('col'))]
    all_to_all x1 -> x2, blocking collectives: 14.3 us -> 25.4 us  [from_everyone(): return lax.all_to_all(copies, axis, split_axis=0, concat_axis=0, tiled=True)]
  transfers between devices with their start and end apart: 3 -> 3, of which waited for: 3 -> 3; matrix products, arithmetic and copies ran while one was open for 18% -> 3% of each run, Pallas kernels for 0% -> 0%
where the time goes in v1:
time: 697 us; the launch traced here: 694 us
  waiting for transfers between devices  535 us (77%)
  matrix products  67.1 us (10%)
  local copies, waits for them, and re-layouts  38.3 us (5%)
  blocking collectives  25.4 us (4%)
  starting transfers between devices  22.6 us (3%)
    all_to_all x2, waiting for transfers between devices, per_device(): lax.all_to_all(jnp.stack([reflectors[owners[panel]]] * lax.axis_size('col...  525 us
    dot_general x6, matrix products, hdot(): jnp.dot(left, right, precision=lax.Precision.HIGHEST, preferred_element_t...  67.1 us
    all_to_all x2, blocking collectives, from_everyone(): return lax.all_to_all(copies, axis, split_axis=0, concat_axis=0, tiled=True)  25.4 us
    all_to_all x2, starting transfers between devices, per_device(): lax.all_to_all(jnp.stack([reflectors[owners[panel]]] * lax.axis_size('col...  16.7 us
    another operation x2, local copies, waits for them, and re-layouts, per_device(): jnp.stack([reflectors[owners[panel]]] * lax.axis_size('col'))  15.5 us
  transfers between devices with their start and end apart: 3, of which 3 were waited for; matrix products, arithmetic and copies ran while one was open for 3% of the time, Pallas kernels for 0%

profile of v1, /device:TPU:0, one launch (start us, length us, event | category | flops | bytes accessed | tf_op | source)
XLA Modules:
  0.0 694.3 jit_solution(96758718015251292)
XLA Ops:
  0.0 1.1 reshape.28
  1.1 0.5 and_reduce_fusion
  1.6 0.2 reduce.1
  1.9 3.6 reshape.29
  5.4 2.9 copy.15
  8.4 8.0 %gather_fusion = f32[1024,4,64]{2,1,0:T(4,128)} fusion(f32[4,1024,64]{2,0,1:T(4,128)S(1)} %copy.15, s32[1024]{0:T(1024)S(1)} %broadcast_clamp_fusion), kind=kCustom, calls=%fused_computation | custom fusion | bytes 2101248 | tf_op jit(solution)/shard_map/jit(_take)/gather | solution.py:31
  16.3 1.7 copy.16
  18.1 0.7 gather.7
  18.7 0.2 broadcast_in_dim.28
  18.9 0.2 broadcast_in_dim.29
  19.2 0.1 broadcast_select_fusion
  19.3 1.6 copy.17
  20.9 5.9 all-to-all-start
  26.9 0.7 fusion.12
  31.3 1.7 dynamic-slice_bitcast_fusion
  33.0 9.8 %all-to-all-done = f32[4,8,8192]{2,0,1:T(4,128)S(1)} async-done(((f32[4,8,8192]{2,0,1:T(4,128)}), f32[4,8,8192]{2,0,1:T(4,128)S(1)}, u32[]{:S(2)}, u32[]{:S(2)}) %all-to-all-start) | async-done | bytes 1048608 | tf_op jit(solution)/shard_map/all_to_all | solution.py:32
  42.8 7.7 %stack.6 = f32[16,32,8192]{2,1,0:T(8,128)} broadcast(f32[32,8192]{1,0:T(8,128)S(1)} %get-tuple-element.8), dimensions={1,2} | broadcast | bytes 17825792 | tf_op jit(solution)/shard_map/stack | solution.py:37
  50.5 7.5 %all-to-all-start.1 = ((f32[16,32,8192]{2,1,0:T(8,128)}), f32[16,32,8192]{2,1,0:T(8,128)}, u32[]{:S(2)}, u32[]{:S(2)}) async-start(f32[16,32,8192]{2,1,0:T(8,128)} %stack.6), calls=%async_computation.1 | async-start | bytes 33554432 | tf_op jit(solution)/shard_map/all_to_all | solution.py:36
  58.0 0.4 reshape.30
  58.4 270.0 %all-to-all-done.1 = f32[16,32,8192]{2,1,0:T(8,128)} async-done(((f32[16,32,8192]{2,1,0:T(8,128)}), f32[16,32,8192]{2,1,0:T(8,128)}, u32[]{:S(2)}, u32[]{:S(2)}) %all-to-all-start.1) | async-done | bytes 16777248 | tf_op jit(solution)/shard_map/all_to_all | solution.py:36
  328.3 18.1 %fusion.13 = f32[32,512]{1,0:T(8,128)S(1)} fusion(f32[32,8192]{1,0:T(8,128)S(1)} %reshape.30, f32[512,8192]{1,0:T(8,128)} %bitcast.5), kind=kOutput, calls=%fused_computation.31 | convolution fusion | flops 1610612736 | bytes 17891328 | tf_op jit(solution)/shard_map/dot_general | solution.py:20
  346.5 13.2 %all_to_all.35 = f32[8,32,512]{2,1,0:T(8,128)} all-to-all(f32[8,32,512]{2,1,0:T(8,128)S(1)} %broadcast_in_dim.32), channel_id=1, replica_groups=mesh['row'=8,'col'=16] {'row'}, dimensions={0} | all-to-all | bytes 1048576 | tf_op jit(solution)/shard_map/all_to_all | solution.py:12
  359.7 7.7 %stack.7 = f32[16,32,8192]{2,1,0:T(8,128)} broadcast(f32[32,8192]{1,0:T(8,128)S(1)} %get-tuple-element.7), dimensions={1,2} | broadcast | bytes 17825792 | tf_op jit(solution)/shard_map/stack | solution.py:37
  367.4 9.2 %all-to-all-start.3 = ((f32[16,32,8192]{2,1,0:T(8,128)}), f32[16,32,8192]{2,1,0:T(8,128)}, u32[]{:S(2)}, u32[]{:S(2)}) async-start(f32[16,32,8192]{2,1,0:T(8,128)} %stack.7), calls=%async_computation.3 | async-start | bytes 33554432 | tf_op jit(solution)/shard_map/all_to_all | solution.py:36
  376.6 1.1 reduce_sum.18
  377.7 1.1 fusion.1
  378.8 13.2 %convolution_subtract_fusion.1 = f32[32,8192]{1,0:T(8,128)S(1)} fusion(f32[32,8192]{1,0:T(8,128)S(1)} %reshape.30, f32[32,512]{1,0:T(8,128)S(1)} %fusion.1, f32[512,8192]{1,0:T(8,128)} %bitcast.5), kind=kOutput, calls=%fused_computation.2 | convolution fusion | flops 1610874880 | bytes 18939904 | tf_op jit(solution)/shard_map/dot_general | solution.py:20
  392.0 255.2 %all-to-all-done.3 = f32[16,32,8192]{2,1,0:T(8,128)} async-done(((f32[16,32,8192]{2,1,0:T(8,128)}), f32[16,32,8192]{2,1,0:T(8,128)}, u32[]{:S(2)}, u32[]{:S(2)}) %all-to-all-start.3) | async-done | bytes 16777248 | tf_op jit(solution)/shard_map/all_to_all | solution.py:36
  647.2 18.1 %fusion.14 = f32[32,512]{1,0:T(8,128)S(1)} fusion(f32[32,8192]{1,0:T(8,128)S(1)} %convolution_subtract_fusion.1, f32[512,8192]{1,0:T(8,128)} %bitcast.9), kind=kOutput, calls=%fused_computation.32 | convolution fusion | flops 1610612736 | bytes 17891328 | tf_op jit(solution)/shard_map/dot_general | solution.py:20
  665.4 12.2 %all_to_all.36 = f32[8,32,512]{2,1,0:T(8,128)S(1)} all-to-all(f32[8,32,512]{2,1,0:T(8,128)S(1)} %broadcast_in_dim.34), channel_id=1, replica_groups=mesh['row'=8,'col'=16] {'row'}, dimensions={0} | all-to-all | bytes 1048576 | tf_op jit(solution)/shard_map/all_to_all | solution.py:12
  677.7 2.4 fusion
  680.1 14.2 %convolution_subtract_fusion = f32[32,8192]{1,0:T(8,128)} fusion(f32[32,8192]{1,0:T(8,128)S(1)} %convolution_subtract_fusion.1, f32[32,512]{1,0:T(8,128)S(1)} %fusion, f32[512,8192]{1,0:T(8,128)} %bitcast.9), kind=kOutput, calls=%fused_computation.1 | convolution fusion | flops 1610874880 | bytes 18939904 | tf_op jit(solution)/shard_map/dot_general | solution.py:20
  (9 shorter events, 0.2 us)
Async XLA Ops:
  0.0 26.8 %copy-start.1 = (s32[16]{0:T(128)S(1)}, s32[16]{0:T(128)}, u32[]{:S(2)}) copy-start(s32[16]{0:T(128)} %param.9) | copy-start | bytes 196
  20.9 21.8 %all-to-all-start = ((f32[4,8,8192]{2,0,1:T(4,128)}), f32[4,8,8192]{2,0,1:T(4,128)S(1)}, u32[]{:S(2)}, u32[]{:S(2)}) async-start(f32[4,8,8192]{2,0,1:T(4,128)} %copy.17), calls=%async_computation | async-start | bytes 2097152 | tf_op jit(solution)/shard_map/all_to_all | solution.py:32
  50.5 277.8 %all-to-all-start.1 = ((f32[16,32,8192]{2,1,0:T(8,128)}), f32[16,32,8192]{2,1,0:T(8,128)}, u32[]{:S(2)}, u32[]{:S(2)}) async-start(f32[16,32,8192]{2,1,0:T(8,128)} %stack.6), calls=%async_computation.1 | async-start | bytes 33554432 | tf_op jit(solution)/shard_map/all_to_all | solution.py:36
  367.4 10.3 %copy-start = (f32[2,512,512]{2,1,0:T(8,128)S(1)}, f32[2,512,512]{2,1,0:T(8,128)}, u32[]{:S(2)}) copy-start(f32[2,512,512]{2,1,0:T(8,128)} %param.8) | copy-start | bytes 6291460
  367.4 279.8 %all-to-all-start.3 = ((f32[16,32,8192]{2,1,0:T(8,128)}), f32[16,32,8192]{2,1,0:T(8,128)}, u32[]{:S(2)}, u32[]{:S(2)}) async-start(f32[16,32,8192]{2,1,0:T(8,128)} %stack.7), calls=%async_computation.3 | async-start | bytes 33554432 | tf_op jit(solution)/shard_map/all_to_all | solution.py:36
